TPU v7x, 32 devices: a whole 2x2x4 slice. The times are simulated.
32 devices in a mesh: gx: 2 (over y), gy: 4 (over x, core), gz: 4 (over z).
Axes of the slice: x: 2, y: 2, z: 4, core: 2. Of those that a mesh axis runs over, the one named last changes fastest.
Arguments:
- wavefunctions: bfloat16 [32, 64, 64, 128], P('gx', 'gy', 'gz'), may hold values from -512 to 512, as said below
- potential: float32 [32, 64, 64], P('gx', 'gy', 'gz'), may hold values from 0 to 3
Outputs:
- rotated: float32 [32, 64, 64, 128], P('gx', 'gy', 'gz')
- residual: bfloat16 [32, 64, 64, 128], P('gx', 'gy', 'gz')
- quotients: float32 [128], replicated
- norms: float32 [128], replicated
Inputs may be any that keep to these rules, and one draw needn't show every extreme that they name: `wavefunctions`: real values mixed across bands, of full rank.
All inputs are finite; a program needn't handle non-finite values.
Results may differ from a plain program's by a relative error of at most 0.0007.
Values may be sent and summed in bfloat16 or wider, within the bound.
A program may use at most 64 MiB of HBM per device.

v0:
```python
import jax
import jax.numpy as jnp
from jax import lax
from jax.sharding import PartitionSpec as P


def extended(block, sides, width):
    for axis, dim in sides:
        count = lax.axis_size(axis)
        forward = [(i, i + 1) for i in range(count - 1)]
        forward.append((count - 1, 0))
        backward = [(target, source) for source, target in forward]
        low = lax.ppermute(
            lax.slice_in_dim(block, block.shape[dim] - width, None, axis=dim), axis, forward
        )
        high = lax.ppermute(lax.slice_in_dim(block, 0, width, axis=dim), axis, backward)
        block = jnp.concatenate([low, block, high], axis=dim)
    return block


def stencil(padded, center, potential):
    cx, cy, cz = (center.shape[0], center.shape[1], center.shape[2])
    total = -30.0 * 3.0 * center
    weights = ((0, -1.0), (1, 16.0), (3, 16.0), (4, -1.0))
    for offset, weight in weights:
        total = total + weight * padded[offset : offset + cx, 2 : 2 + cy, 2 : 2 + cz]
        total = total + weight * padded[2 : 2 + cx, offset : offset + cy, 2 : 2 + cz]
        total = total + weight * padded[2 : 2 + cx, 2 : 2 + cy, offset : offset + cz]
    return -0.5 * total / 12.0 + potential[..., None] * center


def rotate(field, inverse):
    shape = field.shape
    flat = field.reshape(-1, shape[3])
    return jnp.dot(flat, inverse.T, precision=lax.Precision.HIGHEST).reshape(shape)


def local(wavefunctions, potential):
    cx, cy, cz, bands = wavefunctions.shape
    total_cells = cx * cy * cz * lax.axis_size("gx") * lax.axis_size("gy") * lax.axis_size("gz")
    flat = wavefunctions.reshape(-1, bands)
    local_correlation = lax.dot_general(
        flat, flat, (((0,), (0,)), ((), ())), preferred_element_type=jnp.float32
    )
    correlation = lax.psum(local_correlation, ("gx", "gy", "gz")) / total_cells
    factor = jnp.linalg.cholesky(correlation)
    inverse = lax.linalg.triangular_solve(
        factor, jnp.eye(bands, dtype=jnp.float32), left_side=True, lower=True
    )
    given = wavefunctions.astype(jnp.float32)
    rotated = rotate(given, inverse)
    padded = extended(rotated, (("gx", 0), ("gy", 1), ("gz", 2)), 2)
    applied = stencil(padded, rotated, potential)
    cross = jnp.sum(rotated * applied, axis=(0, 1, 2))
    self_applied = jnp.sum(applied * applied, axis=(0, 1, 2))
    self_rotated = jnp.sum(rotated * rotated, axis=(0, 1, 2))
    cross_all, applied_all, rotated_all = lax.psum(
        (cross, self_applied, self_rotated), ("gx", "gy", "gz")
    )
    quotients = cross_all / total_cells
    squares = applied_all - 2.0 * quotients * cross_all + quotients * quotients * rotated_all
    leftover = applied - quotients * rotated
    norms = jnp.sqrt(squares / total_cells + 1e-06)
    return (rotated, leftover.astype(jnp.bfloat16), quotients, norms)


def solution(mesh):
    placed = (P("gx", "gy", "gz", None), P("gx", "gy", "gz"))
    return jax.shard_map(
        local,
        mesh=mesh,
        in_specs=placed,
        out_specs=(P("gx", "gy", "gz", None), P("gx", "gy", "gz", None), P(), P()),
        check_vma=False,
    )
```

profile of v0, /device:TPU:0, one launch (start us, length us, event | category | flops | bytes accessed | tf_op | source)
XLA Modules:
  0.0 271.0 jit_solution(13407734252116796372)
XLA Ops:
  7.2 1.2 copy-done
  8.4 1.1 convolution_bitcast_fusion.1
  9.5 126.7 %all-reduce.3.cloned.1.call-done = f32[128,128]{0,1:T(8,128)} async-done(((f32[128,128]{0,1:T(8,128)}), f32[128,128]{0,1:T(8,128)}) %all-reduce.3.cloned.1.call-update) | async-done | bytes 65552 | tf_op jit(solution)/shard_map/psum | solution.py:45
  136.3 0.8 broadcast_multiply_fusion
  137.2 0.9 fusion.25
  138.1 11.7 %cholesky.17 = f32[128,128]{1,0:T(8,128)S(1)} custom-call(f32[128,128]{1,0:T(8,128)S(1)} %fusion.25), custom_call_target="Cholesky" | custom-call | tf_op jit(solution)/shard_map/jit(cholesky)/cholesky | solution.py:46
  149.8 0.6 compare_reduce_fusion
  150.5 0.7 fusion.22
  151.1 9.8 %custom-call.6 = f32[1,128,128]{1,2,0:T(8,128)S(1)} custom-call(f32[1,128,128]{2,1,0:T(8,128)S(1)} %fusion.22), custom_call_target="InvertDiagBlocksLowerTriangular" | custom-call | tf_op jit(solution)/shard_map/triangular_solve | solution.py:47
  161.2 1.1 multiply_reduce_fusion
  162.3 1.3 copy-done.2
  163.7 0.8 copy.21
  164.5 0.8 copy.22
  165.3 1.5 collective-permute-start.1
  166.8 0.6 collective-permute-start
  167.4 1.9 copy.20
  169.3 4.7 %collective-permute-done.1 = f32[2,16,16,128]{3,2,1,0:T(8,128)S(1)} collective-permute-done((f32[2,16,16,128]{3,2,1,0:T(8,128)}, f32[2,16,16,128]{3,2,1,0:T(8,128)S(1)}, u32[]{:S(2)}, u32[]{:S(2)}) %collective-permute-start.1) | collective-permute-done | bytes 262176 | tf_op jit(solution)/shard_map/ppermute | solution.py:16
  174.0 5.7 %collective-permute-done = f32[2,16,16,128]{3,2,1,0:T(8,128)} collective-permute-done((f32[2,16,16,128]{3,2,1,0:T(8,128)}, f32[2,16,16,128]{3,2,1,0:T(8,128)}, u32[]{:S(2)}, u32[]{:S(2)}) %collective-permute-start) | collective-permute-done | bytes 262176 | tf_op jit(solution)/shard_map/ppermute | solution.py:13
  179.7 0.8 pad_maximum_fusion.20
  180.5 0.6 collective-permute-start.2
  181.2 1.2 collective-permute-start.3
  182.3 6.5 %collective-permute-done.2 = f32[20,2,16,128]{3,2,1,0:T(8,128)S(1)} collective-permute-done((f32[20,2,16,128]{3,2,1,0:T(8,128)S(1)}, f32[20,2,16,128]{3,2,1,0:T(8,128)S(1)}, u32[]{:S(2)}, u32[]{:S(2)}) %collective-permute-start.2) | collective-permute-done | bytes 327712 | tf_op jit(solution)/shard_map/ppermute | solution.py:13
  188.8 0.7 collective-permute-done.3
  189.6 1.3 pad_maximum_fusion.17
  190.8 1.2 collective-permute-start.4
  192.0 2.7 %collective-permute-start.5 = (f32[20,20,2,128]{3,2,1,0:T(2,128)S(1)}, f32[20,20,2,128]{3,2,1,0:T(2,128)S(1)}, u32[]{:S(2)}, u32[]{:S(2)}) collective-permute-start(f32[20,20,2,128]{3,2,1,0:T(2,128)S(1)} %get-tuple-element.17), channel_id=1, source_target_pairs={{1,0},{2,1},{3,2},{0,3},{5,4},{6,5},{7,6},{4,7},{9,8},{10,9},{11,1... | collective-permute-start | bytes 1228808 | tf_op jit(solution)/shard_map/ppermute | solution.py:16
  194.7 1.6 maximum_maximum_fusion
  196.4 8.7 %collective-permute-done.4 = f32[20,20,2,128]{3,2,1,0:T(2,128)S(1)} collective-permute-done((f32[20,20,2,128]{3,2,1,0:T(2,128)S(1)}, f32[20,20,2,128]{3,2,1,0:T(2,128)S(1)}, u32[]{:S(2)}, u32[]{:S(2)}) %collective-permute-start.4) | collective-permute-done | bytes 409632 | tf_op jit(solution)/shard_map/ppermute | solution.py:13
  205.1 7.6 %collective-permute-done.5 = f32[20,20,2,128]{3,2,1,0:T(2,128)S(1)} collective-permute-done((f32[20,20,2,128]{3,2,1,0:T(2,128)S(1)}, f32[20,20,2,128]{3,2,1,0:T(2,128)S(1)}, u32[]{:S(2)}, u32[]{:S(2)}) %collective-permute-start.5) | collective-permute-done | bytes 409632 | tf_op jit(solution)/shard_map/ppermute | solution.py:16
  212.7 8.0 %multiply_reduce_fusion.1 = (f32[128]{0:T(128)S(1)}, f32[128]{0:T(128)S(1)}, f32[16,16,16,128]{3,2,1,0:T(8,128)}) fusion(f32[16,16,16,128]{3,2,1,0:T(8,128)S(1)} %bitcast.26, f32[16,16,16]{2,1,0:T(8,128)S(1)} %copy-done.3, f32[20,20,2,128]{3,2,1,0:T(2,128)S(1)} %collective-permute-done.5, f32[20,2,16,128]{3,2,1,0:T(8,128)S(1)} %collective-permute-done.3, ...), kind=kLoop, calls=%fused_computation.48 | loop fusion | flops 29359872 | bytes 14599168 | tf_op jit(solution)/shard_map/reduce_sum | solution.py:55
  220.7 40.1 %all-reduce = (f32[128]{0:T(128)S(1)}, f32[128]{0:T(128)S(1)}, f32[128]{0:T(128)S(1)}) all-reduce(f32[128]{0:T(128)S(1)} %get-tuple-element.9, f32[128]{0:T(128)S(1)} %get-tuple-element.24, f32[128]{0:T(128)S(1)} %get-tuple-element.8), channel_id=1, replica_groups=mesh['gx'=2,'gy'=4,'gz'=4] {'gx','gy','gz'}, use_global_device_ids=true, to_apply=%region_4.5 | all-reduce | flops 384 | bytes 3072 | tf_op jit(solution)/shard_map/psum | solution.py:57
  261.3 2.8 %subtract_convert_fusion = bf16[16,16,16,128]{3,2,1,0:T(8,128)(2,1)} fusion(f32[16,16,16,128]{3,2,1,0:T(8,128)} %get-tuple-element.15, f32[128]{0:T(128)S(1)} %get-tuple-element.14, f32[4096,128]{1,0:T(8,128)S(1)} %copy.20), kind=kLoop, calls=%fused_computation.49 | loop fusion | flops 1572864 | bytes 5243392 | tf_op jit(solution)/shard_map/convert_element_type | solution.py:64
  (15 shorter events, 1.0 us)
Async XLA Ops:
  7.2 1.2 copy-start
  7.2 129.1 %all-reduce.3.cloned.1.call-start = ((), (), s32[]{:S(2)}) async-start(), calls=%async_computation | async-start | bytes 131072 | tf_op jit(solution)/shard_map/psum | solution.py:45
  162.3 1.3 copy-start.2
  165.3 8.6 %collective-permute-start.1 = (f32[2,16,16,128]{3,2,1,0:T(8,128)}, f32[2,16,16,128]{3,2,1,0:T(8,128)S(1)}, u32[]{:S(2)}, u32[]{:S(2)}) collective-permute-start(f32[2,16,16,128]{3,2,1,0:T(8,128)} %bitcast.8), channel_id=1, source_target_pairs={{16,0},{0,16},{17,1},{1,17},{18,2},{2,18},{19,3},{3,19},{20,4},{4,... | collective-permute-start | bytes 786440 | tf_op jit(solution)/shard_map/ppermute | solution.py:16
  166.8 12.9 %collective-permute-start = (f32[2,16,16,128]{3,2,1,0:T(8,128)}, f32[2,16,16,128]{3,2,1,0:T(8,128)}, u32[]{:S(2)}, u32[]{:S(2)}) collective-permute-start(f32[2,16,16,128]{3,2,1,0:T(8,128)} %bitcast.7), channel_id=1, source_target_pairs={{0,16},{16,0},{1,17},{17,1},{2,18},{18,2},{3,19},{19,3},{4,20},{20... | collective-permute-start | bytes 786440 | tf_op jit(solution)/shard_map/ppermute | solution.py:13
  169.3 92.0 %copy-start.1 = (f32[4096,128]{1,0:T(8,128)}, f32[4096,128]{1,0:T(8,128)S(1)}, u32[]{:S(2)}) copy-start(f32[4096,128]{1,0:T(8,128)S(1)} %copy.20) | copy-start | bytes 6291460
  180.5 8.3 %collective-permute-start.2 = (f32[20,2,16,128]{3,2,1,0:T(8,128)S(1)}, f32[20,2,16,128]{3,2,1,0:T(8,128)S(1)}, u32[]{:S(2)}, u32[]{:S(2)}) collective-permute-start(f32[20,2,16,128]{3,2,1,0:T(8,128)S(1)} %get-tuple-element.20), channel_id=1, source_target_pairs={{0,4},{4,8},{8,12},{12,0},{1,5},{5,9},{9,13},{13,1},{2,6},{6,10},{... | collective-permute-start | bytes 983048 | tf_op jit(solution)/shard_map/ppermute | solution.py:13
  181.2 8.4 %collective-permute-start.3 = (f32[20,2,16,128]{3,2,1,0:T(8,128)S(1)}, f32[20,2,16,128]{3,2,1,0:T(8,128)S(1)}, u32[]{:S(2)}, u32[]{:S(2)}) collective-permute-start(f32[20,2,16,128]{3,2,1,0:T(8,128)S(1)} %get-tuple-element.21), channel_id=1, source_target_pairs={{4,0},{8,4},{12,8},{0,12},{5,1},{9,5},{13,9},{1,13},{6,2},{10,6},{... | collective-permute-start | bytes 983048 | tf_op jit(solution)/shard_map/ppermute | solution.py:16
  190.8 14.2 %collective-permute-start.4 = (f32[20,20,2,128]{3,2,1,0:T(2,128)S(1)}, f32[20,20,2,128]{3,2,1,0:T(2,128)S(1)}, u32[]{:S(2)}, u32[]{:S(2)}) collective-permute-start(f32[20,20,2,128]{3,2,1,0:T(2,128)S(1)} %get-tuple-element.16), channel_id=1, source_target_pairs={{0,1},{1,2},{2,3},{3,0},{4,5},{5,6},{6,7},{7,4},{8,9},{9,10},{10,1... | collective-permute-start | bytes 1228808 | tf_op jit(solution)/shard_map/ppermute | solution.py:13
  192.0 20.7 %copy-start.3 = (f32[16,16,16]{2,1,0:T(8,128)S(1)}, f32[16,16,16]{2,1,0:T(8,128)}, u32[]{:S(2)}) copy-start(f32[16,16,16]{2,1,0:T(8,128)} %param.3) | copy-start | bytes 49156
  192.0 20.7 %collective-permute-start.5 = (f32[20,20,2,128]{3,2,1,0:T(2,128)S(1)}, f32[20,20,2,128]{3,2,1,0:T(2,128)S(1)}, u32[]{:S(2)}, u32[]{:S(2)}) collective-permute-start(f32[20,20,2,128]{3,2,1,0:T(2,128)S(1)} %get-tuple-element.17), channel_id=1, source_target_pairs={{1,0},{2,1},{3,2},{0,3},{5,4},{6,5},{7,6},{4,7},{9,8},{10,9},{11,1... | collective-permute-start | bytes 1228808 | tf_op jit(solution)/shard_map/ppermute | solution.py:16
  261.3 2.9 %copy-start.4 = (f32[128]{0:T(128)}, f32[128]{0:T(128)S(1)}, u32[]{:S(2)}) copy-start(f32[128]{0:T(128)S(1)} %get-tuple-element.14) | copy-start | bytes 1540
Sparse Core Ops, SparseCore 0:
  14.1 122.0 all-reduce.2
where the time goes:
time: 272 us; the launch traced here: 271 us
  waiting for transfers between devices  161 us (59%)
  blocking collectives  40.1 us (15%)
  other arithmetic  39.6 us (15%)
  between operations  14.1 us (5%)
  starting transfers between devices  7.74 us (3%)
  local copies, waits for them, and re-layouts  6.19 us (2%)
    psum x1, waiting for transfers between devices, local(): correlation = lax.psum(local_correlation, ('gx', 'gy', 'gz')) / total_cells  127 us
    psum x1, blocking collectives, local(): lax.psum((cross, self_applied, self_rotated), ('gx', 'gy', 'gz'))  40.1 us
    ppermute x3, waiting for transfers between devices, extended(): lax.ppermute(lax.slice_in_dim(block, block.shape[dim] - width, None, axis...  20.9 us
    ppermute x3, waiting for transfers between devices, extended(): lax.ppermute(lax.slice_in_dim(block, 0, width, axis=dim), axis, backward)  13.1 us
    another operation x3, other arithmetic, local(): factor = jnp.linalg.cholesky(correlation)  12.4 us
    another operation x2, other arithmetic, local(): lax.linalg.triangular_solve(factor, jnp.eye(bands, dtype=jnp.float32), le...  10.5 us
    reduce_sum x1, other arithmetic, local(): self_applied = jnp.sum(applied * applied, axis=(0, 1, 2))  8.02 us
  transfers between devices with their start and end apart: 7, of which 7 were waited for; matrix products, arithmetic and copies ran while one was open for 1% of the time, Pallas kernels for 0%

commit v1 on v0

v1 whole, which is shorter than its diff:
```python
import functools

import jax
import jax.numpy as jnp
from jax import lax
from jax.experimental import pallas as pl
from jax.experimental.pallas import tpu as pltpu
from jax.sharding import PartitionSpec as P

MESH = pl.DeviceIdType.MESH
F32 = jnp.float32
BF16 = jnp.bfloat16


def split2(a):
    hi = a.astype(BF16)
    return hi, (a - hi.astype(F32)).astype(BF16)


def split3(a):
    hi = a.astype(BF16)
    rest = a - hi.astype(F32)
    mid = rest.astype(BF16)
    return hi, mid, (rest - mid.astype(F32)).astype(BF16)


def gram(a, b):
    return lax.dot_general(a, b, (((0,), (0,)), ((), ())), preferred_element_type=F32)


def reduce_kernel(sizes, p_any, v_ref, hi_ref, lo_ref, sum_ref,
                  pext, ylo, yhi, zlo, zhi, zsend, part, got1, acc, got2, total, gathered,
                  load_sem, hs, hr, s1, r1, s2, r2, s3, r3):
    nx, ny, nz = sizes
    ne = nx * nz
    cx, cy, cz, bands = p_any.shape
    mx, my, mz = lax.axis_index("gx"), lax.axis_index("gy"), lax.axis_index("gz")
    me = mx * nz + mz

    def line_peer(offset):
        return (mx, lax.rem(my + offset, ny), mz)

    def plane_peer(offset):
        e = lax.rem(me + offset, ne)
        return (e // nz, my, lax.rem(e, nz))

    load = pltpu.make_async_copy(p_any, pext.at[pl.ds(2, cx)], load_sem)
    load.start()
    barrier = pltpu.get_barrier_semaphore()
    for o in range(1, ny):
        pl.semaphore_signal(barrier, inc=1, device_id=line_peer(o), device_id_type=MESH)
    for o in range(1, ne):
        pl.semaphore_signal(barrier, inc=1, device_id=plane_peer(o), device_id_type=MESH)
    load.wait()
    own = pext[2:2 + cx]
    zsend[0] = own[:, :, cz - 2:, :]
    zsend[1] = own[:, :, :2, :]
    pl.semaphore_wait(barrier, ny - 1 + ne - 1)

    def remote(src, dst, i, device):
        return pltpu.make_async_remote_copy(src_ref=src, dst_ref=dst, send_sem=hs.at[i], recv_sem=hr.at[i],
                                            device_id=device, device_id_type=MESH)

    xf = (lax.rem(mx + 1, nx), my, mz)
    xb = (lax.rem(mx + nx - 1, nx), my, mz)
    yf = (mx, lax.rem(my + 1, ny), mz)
    yb = (mx, lax.rem(my + ny - 1, ny), mz)
    zf = (mx, my, lax.rem(mz + 1, nz))
    zb = (mx, my, lax.rem(mz + nz - 1, nz))
    halos = [
        remote(zsend.at[0], zlo, 0, zf),
        remote(zsend.at[1], zhi, 1, zb),
        remote(p_any.at[pl.ds(cx - 2, 2)], pext.at[pl.ds(0, 2)], 2, xf),
        remote(p_any.at[pl.ds(0, 2)], pext.at[pl.ds(cx + 2, 2)], 3, xb),
        remote(p_any.at[:, pl.ds(cy - 2, 2)], ylo, 4, yf),
        remote(p_any.at[:, pl.ds(0, 2)], yhi, 5, yb),
    ]
    for copy in halos:
        copy.start()
    flat = pext[2:2 + cx].reshape(cx * cy * cz, bands)
    rows = bands // ny

    def put(slot, matrix):
        for k in range(ny):
            part[k, slot * rows:(slot + 1) * rows] = matrix[k * rows:(k + 1) * rows]

    put(0, gram(flat, flat))
    for copy in halos:
        copy.wait()

    def plane(i, carry):
        center = pext[i + 2].astype(F32)
        one, two = 16.0 / -24.0, 1.0 / 24.0
        near = pext[i + 1].astype(F32) + pext[i + 3].astype(F32)
        far = pext[i].astype(F32) + pext[i + 4].astype(F32)
        ye = jnp.concatenate([ylo[i].astype(F32), center, yhi[i].astype(F32)], axis=0)
        near = near + (ye[1:1 + cy] + ye[3:3 + cy])
        far = far + (ye[0:cy] + ye[4:4 + cy])
        ze = jnp.concatenate([zlo[i].astype(F32), center, zhi[i].astype(F32)], axis=1)
        near = near + (ze[:, 1:1 + cz] + ze[:, 3:3 + cz])
        far = far + (ze[:, 0:cz] + ze[:, 4:4 + cz])
        level = v_ref[i][:, :, None] + 90.0 / 24.0
        applied = one * near + two * far + level * center
        hi, lo = split2(applied)
        hi_ref[i] = hi
        lo_ref[i] = lo
        return carry

    lax.fori_loop(0, cx, plane, 0)
    hi = hi_ref[...].reshape(cx * cy * cz, bands)
    lo = lo_ref[...].reshape(cx * cy * cz, bands)
    put(1, gram(flat, hi) + gram(flat, lo))
    cross = gram(hi, lo)
    put(2, gram(hi, hi) + cross + cross.T)

    copies = []
    for o in range(1, ny):
        copies.append(pltpu.make_async_remote_copy(
            src_ref=part.at[lax.rem(my + o, ny)], dst_ref=got1.at[o - 1], send_sem=s1.at[o - 1], recv_sem=r1.at[o - 1],
            device_id=line_peer(o), device_id_type=MESH))
        copies[-1].start()
    for copy in copies:
        copy.wait()
    mine = part[my]
    for o in range(1, ny):
        mine = mine + got1[o - 1]
    acc[...] = mine
    copies = []
    for o in range(1, ne):
        copies.append(pltpu.make_async_remote_copy(
            src_ref=acc, dst_ref=got2.at[me], send_sem=s2.at[o - 1], recv_sem=r2.at[o - 1],
            device_id=plane_peer(o), device_id_type=MESH))
        copies[-1].start()
    got2[me] = mine
    for o in range(1, ne):
        copies[o - 1].wait_send()
        pltpu.make_async_remote_copy(
            src_ref=acc, dst_ref=got2.at[lax.rem(me + ne - o, ne)], send_sem=s2.at[o - 1], recv_sem=r2.at[o - 1],
            device_id=plane_peer(o), device_id_type=MESH).wait_recv()
    whole = got2[0]
    for e in range(1, ne):
        whole = whole + got2[e]
    total[...] = whole
    copies = []
    for o in range(1, ny):
        copies.append(pltpu.make_async_remote_copy(
            src_ref=total, dst_ref=gathered.at[my], send_sem=s3.at[o - 1], recv_sem=r3.at[o - 1],
            device_id=line_peer(o), device_id_type=MESH))
        copies[-1].start()
    gathered[my] = whole
    for o in range(1, ny):
        copies[o - 1].wait_send()
        pltpu.make_async_remote_copy(
            src_ref=total, dst_ref=gathered.at[lax.rem(my + ny - o, ny)], send_sem=s3.at[o - 1], recv_sem=r3.at[o - 1],
            device_id=line_peer(o), device_id_type=MESH).wait_recv()
    for k in range(ny):
        for slot in range(3):
            sum_ref[slot, k * rows:(k + 1) * rows] = gathered[k, slot * rows:(slot + 1) * rows]


def invert(matrix):
    n = matrix.shape[0]
    lane = lax.broadcasted_iota(jnp.int32, (1, n), 1)
    lanes8 = lax.broadcasted_iota(jnp.int32, (8, n), 1)
    sub8 = lax.broadcasted_iota(jnp.int32, (8, n), 0)
    tiles = [matrix[8 * t:8 * t + 8] for t in range(n // 8)]
    for j in range(n - 1):
        t0, r = divmod(j, 8)
        row = tiles[t0][r:r + 1]
        scale = 1.0 / row[:, j:j + 1]
        row = jnp.where(lane == j, 1.0, row) * scale
        here = lanes8 == j
        for t in range(t0 if r < 7 else t0 + 1, n // 8):
            column = tiles[t][:, j:j + 1]
            new = jnp.where(here, 0.0, tiles[t]) - column * row
            tiles[t] = jnp.where(sub8 > r, new, tiles[t]) if t == t0 else new
    out = []
    for t in range(n // 8):
        diagonal = lanes8 == sub8 + 8 * t
        pivot = jnp.sum(jnp.where(diagonal, tiles[t], 0.0), axis=1, keepdims=True)
        unit = jnp.where(diagonal, 1.0, jnp.where(lanes8 < sub8 + 8 * t, tiles[t], 0.0))
        out.append(unit * lax.rsqrt(pivot))
    return jnp.concatenate(out, axis=0)


def dot(a, b):
    return jnp.dot(a, b, preferred_element_type=F32)


def finish_kernel(cells, sums_ref, p_ref, hi_ref, lo_ref, rot_ref, res_ref, quo_ref, norm_ref, split):
    bands = p_ref.shape[1]

    @pl.when(pl.program_id(0) == 0)
    def _():
        correlation = sums_ref[0] / cells
        inverse_t = invert(correlation).T
        for i, piece in enumerate(split3(inverse_t)):
            split[:, i * bands:(i + 1) * bands] = piece

        def quadratic(m):
            prod = jnp.dot(m, inverse_t, precision=lax.Precision.HIGHEST, preferred_element_type=F32)
            return jnp.sum(inverse_t * prod, axis=0, keepdims=True)

        rotated_all = quadratic(sums_ref[0])
        cross_all = quadratic(sums_ref[1])
        applied_all = quadratic(sums_ref[2])
        quotients = cross_all / cells
        squares = applied_all - 2.0 * quotients * cross_all + quotients * quotients * rotated_all
        quo_ref[...] = quotients
        norm_ref[...] = jnp.sqrt(squares / cells + 1e-06)

    p = p_ref[...]
    wide = dot(p, split[:, :2 * bands])
    rotated = wide[:, :bands] + (wide[:, bands:] + dot(p, split[:, 2 * bands:]))
    rot_ref[...] = rotated
    wide = dot(hi_ref[...], split[:, :2 * bands])
    applied = wide[:, :bands] + (wide[:, bands:] + dot(lo_ref[...], split[:, :bands]))
    res_ref[...] = (applied - quo_ref[...] * rotated).astype(BF16)


def local(sizes, wavefunctions, potential):
    nx, ny, nz = sizes
    ne = nx * nz
    cx, cy, cz, bands = wavefunctions.shape
    mine = cx * cy * cz
    rows = 3 * bands // ny
    vmem = pl.BlockSpec(memory_space=pltpu.VMEM)
    dma = pltpu.SemaphoreType.DMA
    hi, lo, sums = pl.pallas_call(
        functools.partial(reduce_kernel, sizes),
        out_shape=(
            jax.ShapeDtypeStruct(wavefunctions.shape, BF16),
            jax.ShapeDtypeStruct(wavefunctions.shape, BF16),
            jax.ShapeDtypeStruct((3, bands, bands), F32),
        ),
        in_specs=[pl.BlockSpec(memory_space=pl.ANY), vmem],
        out_specs=(vmem, vmem, vmem),
        scratch_shapes=[
            pltpu.VMEM((cx + 4, cy, cz, bands), BF16),
            pltpu.VMEM((cx, 2, cz, bands), BF16),
            pltpu.VMEM((cx, 2, cz, bands), BF16),
            pltpu.VMEM((cx, cy, 2, bands), BF16),
            pltpu.VMEM((cx, cy, 2, bands), BF16),
            pltpu.VMEM((2, cx, cy, 2, bands), BF16),
            pltpu.VMEM((ny, rows, bands), F32),
            pltpu.VMEM((ny - 1, rows, bands), F32),
            pltpu.VMEM((rows, bands), F32),
            pltpu.VMEM((ne, rows, bands), F32),
            pltpu.VMEM((rows, bands), F32),
            pltpu.VMEM((ny, rows, bands), F32),
            dma, dma((6,)), dma((6,)),
            dma((ny - 1,)), dma((ny - 1,)), dma((ne - 1,)), dma((ne - 1,)), dma((ny - 1,)), dma((ny - 1,)),
        ],
        compiler_params=pltpu.CompilerParams(collective_id=0, has_side_effects=True, vmem_limit_bytes=48 * 1024 * 1024),
    )(wavefunctions, potential)
    steps = 8 if mine % 128 == 0 else 1
    tile = mine // steps
    block = pl.BlockSpec((tile, bands), lambda i: (i, 0))
    line = pl.BlockSpec((1, bands), lambda i: (0, 0))
    rotated, residual, quotients, norms = pl.pallas_call(
        functools.partial(finish_kernel, float(mine * nx * ny * nz)),
        grid=(steps,),
        out_shape=(
            jax.ShapeDtypeStruct((mine, bands), F32),
            jax.ShapeDtypeStruct((mine, bands), BF16),
            jax.ShapeDtypeStruct((1, bands), F32),
            jax.ShapeDtypeStruct((1, bands), F32),
        ),
        in_specs=[pl.BlockSpec((3, bands, bands), lambda i: (0, 0, 0)), block, block, block],
        out_specs=(block, block, line, line),
        scratch_shapes=[pltpu.VMEM((bands, 3 * bands), BF16)],
        compiler_params=pltpu.CompilerParams(vmem_limit_bytes=48 * 1024 * 1024),
    )(sums, wavefunctions.reshape(mine, bands), hi.reshape(mine, bands), lo.reshape(mine, bands))
    shape = wavefunctions.shape
    return rotated.reshape(shape), residual.reshape(shape), quotients.reshape(bands), norms.reshape(bands)


def solution(mesh):
    sizes = (mesh.shape["gx"], mesh.shape["gy"], mesh.shape["gz"])
    placed = (P("gx", "gy", "gz", None), P("gx", "gy", "gz"))
    return jax.shard_map(
        functools.partial(local, sizes),
        mesh=mesh,
        in_specs=placed,
        out_specs=(P("gx", "gy", "gz", None), P("gx", "gy", "gz", None), P(), P()),
        check_vma=False,
    )
```

time: 272 us -> 51.9 us (0.19)
  waiting for transfers between devices: 161 us -> 0 us
  Pallas kernels: 0 us -> 48.9 us
  blocking collectives: 40.1 us -> 0 us
  other arithmetic: 39.6 us -> 0 us
  between operations: 14.1 us -> 0.65 us
  starting transfers between devices: 7.74 us -> 0 us
  local copies, waits for them, and re-layouts: 6.19 us -> 2.12 us
    psum x1 -> x0, waiting for transfers between devices: 127 us -> none  [local(): correlation = lax.psum(local_correlation, ('gx', 'gy', 'gz')) / total_cells]
    pallas_call x0 -> x2, Pallas kernels: none -> 48.9 us  [the longest x1 33.2 us: local(): pl.pallas_call(functools.partial(reduce_kernel, sizes), out_shape=(jax.Sh...]
    psum x1 -> x0, blocking collectives: 40.1 us -> none  [local(): lax.psum((cross, self_applied, self_rotated), ('gx', 'gy', 'gz'))]
    ppermute x6 -> x0, waiting for transfers between devices: 34 us -> none  [the longest x3 20.9 us: extended(): lax.ppermute(lax.slice_in_dim(block, block.shape[dim] - width, None, axis...]
    another operation x5 -> x0, other arithmetic: 22.9 us -> none  [the longest x3 12.4 us: local(): factor = jnp.linalg.cholesky(correlation)]
    reduce_sum x1 -> x0, other arithmetic: 8.02 us -> none  [local(): self_applied = jnp.sum(applied * applied, axis=(0, 1, 2))]
    ppermute x6 -> x0, starting transfers between devices: 7.7 us -> none  [the longest x3 5.36 us: extended(): lax.ppermute(lax.slice_in_dim(block, 0, width, axis=dim), axis, backward)]
    convert_element_type x1 -> x0, other arithmetic: 2.84 us -> none  [local(): return (rotated, leftover.astype(jnp.bfloat16), quotients, norms)]
  transfers between devices with their start and end apart: 7 -> 0, of which waited for: 7 -> 0; matrix products, arithmetic and copies ran while one was open for 1% -> 0% of each run, Pallas kernels for 0% -> 0%
where the time goes in v1:
time: 51.9 us; the launch traced here: 51.7 us
  Pallas kernels  48.9 us (94%)
  local copies, waits for them, and re-layouts  2.12 us (4%)
  between operations  0.65 us (1%)
    pallas_call x1, Pallas kernels, local(): pl.pallas_call(functools.partial(reduce_kernel, sizes), out_shape=(jax.Sh...  33.2 us
    pallas_call x1, Pallas kernels, local(): pl.pallas_call(functools.partial(finish_kernel, float(mine * nx * ny * nz...  15.7 us
    unnamed x4, local copies, waits for them, and re-layouts  2.12 us

profile of v1, /device:TPU:0, one launch (start us, length us, event | category | flops | bytes accessed | tf_op | source)
XLA Modules:
  0.0 51.7 jit_solution(9557743029683270449)
XLA Ops:
  0.6 0.0 copy-start
  0.6 1.2 %copy-done = bf16[16,16,16,128]{3,2,1,0:T(8,128)(2,1)S(1)} copy-done((bf16[16,16,16,128]{3,2,1,0:T(8,128)(2,1)S(1)}, bf16[16,16,16,128]{3,2,1,0:T(8,128)(2,1)}, u32[]{:S(2)}) %copy-start) | copy-done | bytes 1048600
  1.9 0.0 copy-start.1
  1.9 0.9 %copy-done.1 = f32[16,16,16]{2,1,0:T(8,128)S(1)} copy-done((f32[16,16,16]{2,1,0:T(8,128)S(1)}, f32[16,16,16]{2,1,0:T(8,128)}, u32[]{:S(2)}) %copy-start.1) | copy-done | bytes 16408
  2.8 33.2 %shard_map.57 = (bf16[16,16,16,128]{3,2,1,0:T(8,128)(2,1)S(1)}, bf16[16,16,16,128]{3,2,1,0:T(8,128)(2,1)S(1)}, f32[3,128,128]{2,1,0:T(8,128)S(1)}) custom-call(bf16[16,16,16,128]{3,2,1,0:T(8,128)(2,1)S(1)} %copy-done, f32[16,16,16]{2,1,0:T(8,128)S(1)} %copy-done.1), custom_call_target="tpu_custom_call" | custom-call | tf_op jit(solution)/shard_map/pallas_call | solution.py:229
  36.0 15.7 %shard_map.58 = (f32[4096,128]{1,0:T(8,128)}, bf16[4096,128]{1,0:T(8,128)(2,1)}, f32[1,128]{1,0:T(1,128)}, f32[1,128]{1,0:T(1,128)}) custom-call(f32[3,128,128]{2,1,0:T(8,128)S(1)} %get-tuple-element.11.sums_ref, bf16[4096,128]{1,0:T(8,128)(2,1)S(1)} %bitcast.7, bf16[4096,128]{1,0:T(8,128)(2,1)S(1)} %bitcast.8, bf16[4096,128]{1,0:T(8,128)(2,1)S(1)} %bitcast.9), custom_call_target="tpu_custom_call" | custom-call | tf_op jit(solution)/shard_map/pallas_call | solution.py:260
Async XLA Ops:
  0.6 1.2 %copy-start = (bf16[16,16,16,128]{3,2,1,0:T(8,128)(2,1)S(1)}, bf16[16,16,16,128]{3,2,1,0:T(8,128)(2,1)}, u32[]{:S(2)}) copy-start(bf16[16,16,16,128]{3,2,1,0:T(8,128)(2,1)} %p_any.1) | copy-start | bytes 3145732
  1.9 0.9 %copy-start.1 = (f32[16,16,16]{2,1,0:T(8,128)S(1)}, f32[16,16,16]{2,1,0:T(8,128)}, u32[]{:S(2)}) copy-start(f32[16,16,16]{2,1,0:T(8,128)} %v_ref.1) | copy-start | bytes 49156

commit v2 on v1

v2 whole, which is shorter than its diff:
```python
import functools

import jax
import jax.numpy as jnp
from jax import lax
from jax.experimental import pallas as pl
from jax.experimental.pallas import tpu as pltpu
from jax.sharding import PartitionSpec as P

MESH = pl.DeviceIdType.MESH
F32 = jnp.float32
BF16 = jnp.bfloat16


def split2(a):
    hi = a.astype(BF16)
    return hi, (a - hi.astype(F32)).astype(BF16)


def split3(a):
    hi = a.astype(BF16)
    rest = a - hi.astype(F32)
    mid = rest.astype(BF16)
    return hi, mid, (rest - mid.astype(F32)).astype(BF16)


def gram(a, b):
    return lax.dot_general(a, b, (((0,), (0,)), ((), ())), preferred_element_type=F32)


class Reduce:
    def __init__(self, sizes, refs):
        self.part, self.got1, self.acc, self.got2, self.total, self.gathered = refs[:6]
        self.s1, self.r1, self.s2, self.r2, self.s3, self.r3 = refs[6:]
        self.nx, self.ny, self.nz = sizes
        self.ne = self.nx * self.nz
        self.mx, self.my, self.mz = lax.axis_index("gx"), lax.axis_index("gy"), lax.axis_index("gz")
        self.me = self.mx * self.nz + self.mz

    def line_peer(self, offset):
        return (self.mx, lax.rem(self.my + offset, self.ny), self.mz)

    def plane_peer(self, offset):
        e = lax.rem(self.me + offset, self.ne)
        return (e // self.nz, self.my, lax.rem(e, self.nz))

    def scatter_copy(self, o):
        return pltpu.make_async_remote_copy(
            src_ref=self.part.at[lax.rem(self.my + o, self.ny)], dst_ref=self.got1.at[o - 1],
            send_sem=self.s1.at[o - 1], recv_sem=self.r1.at[o - 1],
            device_id=self.line_peer(o), device_id_type=MESH)

    def exchange_copy(self, o, slot):
        return pltpu.make_async_remote_copy(
            src_ref=self.acc, dst_ref=self.got2.at[slot], send_sem=self.s2.at[o - 1], recv_sem=self.r2.at[o - 1],
            device_id=self.plane_peer(o), device_id_type=MESH)

    def gather_copy(self, o, slot):
        return pltpu.make_async_remote_copy(
            src_ref=self.total, dst_ref=self.gathered.at[slot], send_sem=self.s3.at[o - 1], recv_sem=self.r3.at[o - 1],
            device_id=self.line_peer(o), device_id_type=MESH)

    def scatter(self):
        for o in range(1, self.ny):
            self.scatter_copy(o).start()

    def exchange(self):
        for o in range(1, self.ny):
            self.scatter_copy(o).wait()
        mine = self.part[self.my]
        for o in range(1, self.ny):
            mine = mine + self.got1[o - 1]
        self.acc[...] = mine
        for o in range(1, self.ne):
            self.exchange_copy(o, self.me).start()
        self.got2[self.me] = mine

    def gather(self):
        for o in range(1, self.ne):
            self.exchange_copy(o, self.me).wait_send()
            self.exchange_copy(o, lax.rem(self.me + self.ne - o, self.ne)).wait_recv()
        whole = self.got2[0]
        for e in range(1, self.ne):
            whole = whole + self.got2[e]
        self.total[...] = whole
        for o in range(1, self.ny):
            self.gather_copy(o, self.my).start()
        self.gathered[self.my] = whole

    def finish(self):
        for o in range(1, self.ny):
            self.gather_copy(o, self.my).wait_send()
            self.gather_copy(o, lax.rem(self.my + self.ny - o, self.ny)).wait_recv()


def reduce_scratch(sizes, rows, bands):
    nx, ny, nz = sizes
    ne = nx * nz
    dma = pltpu.SemaphoreType.DMA
    chunk = rows // ny
    shapes = ((ny, chunk), (ny - 1, chunk), (chunk,), (ne, chunk), (chunk,), (ny, chunk))
    return [pltpu.VMEM(shape + (bands,), F32) for shape in shapes] + [dma((k - 1,)) for k in (ny, ny, ne, ne, ny, ny)]


def eliminate(tiles, t):
    n = tiles[0].shape[1]
    base = 8 * t
    lane = lax.broadcasted_iota(jnp.int32, (1, n), 1)
    lanes8 = lax.broadcasted_iota(jnp.int32, (8, n), 1)
    sub8 = lax.broadcasted_iota(jnp.int32, (8, n), 0)
    pivots = tiles[t]
    out = jnp.zeros((8, n), F32)
    columns = [jnp.broadcast_to(pivots[:, base + k:base + k + 1], (8, n)) for k in range(8)]
    for k in range(8):
        j = base + k
        pivot = columns[k][k:k + 1]
        scale = 1.0 / pivot
        row = jnp.where(lane == j, 1.0, pivots[k:k + 1])
        out = jnp.where(sub8 == k, jnp.where(lane <= j, row, 0.0) * lax.rsqrt(pivot), out)
        scaled = row * scale
        pivots = jnp.where(sub8 == k, scaled, jnp.where(lanes8 == j, 0.0, pivots) - columns[k] * scaled)
        for later in range(k + 1, 8):
            ratio = columns[later][k:k + 1] * scale
            columns[later] = jnp.where(sub8 == k, ratio, columns[later] - columns[k] * ratio)
    inside = (lanes8 >= base) & (lanes8 < base + 8)
    rest = list(tiles)
    for u in range(t + 1, n // 8):
        old = tiles[u]
        terms = [jnp.broadcast_to(old[:, base + k:base + k + 1], (8, n)) * pivots[k:k + 1] for k in range(8)]
        while len(terms) > 1:
            terms = [terms[i] + terms[i + 1] for i in range(0, len(terms), 2)]
        rest[u] = jnp.where(inside, 0.0, old) - terms[0]
    return out, rest


def reduce_kernel(sizes, cells, p_any, v_any, hi_ref, lo_ref, split_ref, stats_ref,
                  pext, vbuf, ylo, yhi, zlo, zhi, zsend, load_sem, hs, hr, *refs):
    nx, ny, nz = sizes
    ne = nx * nz
    cx, cy, cz, bands = p_any.shape
    first, second = Reduce(sizes, refs[:12]), Reduce(sizes, refs[12:])
    mx, my, mz = first.mx, first.my, first.mz

    load = pltpu.make_async_copy(p_any, pext.at[pl.ds(2, cx)], load_sem.at[0])
    load.start()
    load_v = pltpu.make_async_copy(v_any, vbuf, load_sem.at[1])
    load_v.start()
    barrier = pltpu.get_barrier_semaphore()
    for o in range(1, ny):
        pl.semaphore_signal(barrier, inc=1, device_id=first.line_peer(o), device_id_type=MESH)
    for o in range(1, ne):
        pl.semaphore_signal(barrier, inc=1, device_id=first.plane_peer(o), device_id_type=MESH)
    load.wait()
    own = pext[2:2 + cx]
    zsend[0] = own[:, :, cz - 2:, :]
    zsend[1] = own[:, :, :2, :]
    flat = own.reshape(cx * cy * cz, bands)
    rows = bands // ny

    def put(where, slot, matrix):
        for k in range(ny):
            where[k, slot * rows:(slot + 1) * rows] = matrix[k * rows:(k + 1) * rows]

    put(first.part, 0, gram(flat, flat))
    pl.semaphore_wait(barrier, ny - 1 + ne - 1)

    def remote(src, dst, i, device):
        return pltpu.make_async_remote_copy(src_ref=src, dst_ref=dst, send_sem=hs.at[i], recv_sem=hr.at[i],
                                            device_id=device, device_id_type=MESH)

    xf = (lax.rem(mx + 1, nx), my, mz)
    xb = (lax.rem(mx + nx - 1, nx), my, mz)
    yf = (mx, lax.rem(my + 1, ny), mz)
    yb = (mx, lax.rem(my + ny - 1, ny), mz)
    zf = (mx, my, lax.rem(mz + 1, nz))
    zb = (mx, my, lax.rem(mz + nz - 1, nz))
    halos = [
        remote(zsend.at[0], zlo, 0, zf),
        remote(zsend.at[1], zhi, 1, zb),
        remote(pext.at[pl.ds(cx, 2)], pext.at[pl.ds(0, 2)], 2, xf),
        remote(pext.at[pl.ds(2, 2)], pext.at[pl.ds(cx + 2, 2)], 3, xb),
        remote(pext.at[pl.ds(2, cx), pl.ds(cy - 2, 2)], ylo, 4, yf),
        remote(pext.at[pl.ds(2, cx), pl.ds(0, 2)], yhi, 5, yb),
    ]
    first.scatter()
    for copy in halos:
        copy.start()
    load_v.wait()
    first.exchange()
    for copy in halos:
        copy.wait()

    def plane(i, carry):
        center = pext[i + 2].astype(F32)
        one, two = 16.0 / -24.0, 1.0 / 24.0
        near = pext[i + 1].astype(F32) + pext[i + 3].astype(F32)
        far = pext[i].astype(F32) + pext[i + 4].astype(F32)
        ye = jnp.concatenate([ylo[i].astype(F32), center, yhi[i].astype(F32)], axis=0)
        near = near + (ye[1:1 + cy] + ye[3:3 + cy])
        far = far + (ye[0:cy] + ye[4:4 + cy])
        ze = jnp.concatenate([zlo[i].astype(F32), center, zhi[i].astype(F32)], axis=1)
        near = near + (ze[:, 1:1 + cz] + ze[:, 3:3 + cz])
        far = far + (ze[:, 0:cz] + ze[:, 4:4 + cz])
        level = vbuf[i][:, :, None] + 90.0 / 24.0
        applied = one * near + two * far + level * center
        hi, lo = split2(applied)
        hi_ref[i] = hi
        lo_ref[i] = lo
        return carry

    lax.fori_loop(0, cx, plane, 0)
    flat = pext[2:2 + cx].reshape(cx * cy * cz, bands)
    hi = hi_ref[...].reshape(cx * cy * cz, bands)
    lo = lo_ref[...].reshape(cx * cy * cz, bands)
    put(second.part, 0, gram(flat, hi) + gram(flat, lo))
    cross = gram(hi, lo)
    put(second.part, 1, gram(hi, hi) + cross + cross.T)
    second.scatter()
    first.gather()
    second.exchange()
    first.finish()

    correlation = first.gathered[...].reshape(bands, bands)
    matrix = correlation / cells
    count = bands // 8
    tiles = [matrix[8 * t:8 * t + 8] for t in range(count)]
    inverse = []
    for t in range(count):
        if t == count * 3 // 4:
            second.gather()
        out, tiles = eliminate(tiles, t)
        inverse.append(out)
    inverse_t = jnp.concatenate(inverse, axis=0).T
    for i, piece in enumerate(split3(inverse_t)):
        split_ref[:, i * bands:(i + 1) * bands] = piece
    second.finish()

    def quadratic(m):
        prod = jnp.dot(m, inverse_t, precision=lax.Precision.HIGHEST, preferred_element_type=F32)
        return jnp.sum(inverse_t * prod, axis=0, keepdims=True)

    rotated_all = quadratic(correlation)
    cross_all = quadratic(second.gathered[:, :rows].reshape(bands, bands))
    applied_all = quadratic(second.gathered[:, rows:].reshape(bands, bands))
    quotients = cross_all / cells
    squares = applied_all - 2.0 * quotients * cross_all + quotients * quotients * rotated_all
    stats_ref[0:1] = quotients
    stats_ref[1:2] = jnp.sqrt(squares / cells + 1e-06)


def dot(a, b):
    return jnp.dot(a, b, preferred_element_type=F32)


def finish_kernel(split_ref, stats_ref, p_ref, hi_ref, lo_ref, rot_ref, res_ref, quo_ref, norm_ref):
    bands = p_ref.shape[1]
    split = split_ref[...]
    p = p_ref[...]
    wide = dot(p, split[:, :2 * bands])
    rotated = wide[:, :bands] + (wide[:, bands:] + dot(p, split[:, 2 * bands:]))
    rot_ref[...] = rotated
    wide = dot(hi_ref[...], split[:, :2 * bands])
    applied = wide[:, :bands] + (wide[:, bands:] + dot(lo_ref[...], split[:, :bands]))
    res_ref[...] = (applied - stats_ref[0:1] * rotated).astype(BF16)
    quo_ref[...] = stats_ref[0:1]
    norm_ref[...] = stats_ref[1:2]


def local(sizes, wavefunctions, potential):
    nx, ny, nz = sizes
    cx, cy, cz, bands = wavefunctions.shape
    mine = cx * cy * cz
    vmem = pl.BlockSpec(memory_space=pltpu.VMEM)
    far = pl.BlockSpec(memory_space=pltpu.HBM)
    dma = pltpu.SemaphoreType.DMA
    hi, lo, split, stats = pl.pallas_call(
        functools.partial(reduce_kernel, sizes, float(mine * nx * ny * nz)),
        out_shape=(
            jax.ShapeDtypeStruct(wavefunctions.shape, BF16),
            jax.ShapeDtypeStruct(wavefunctions.shape, BF16),
            jax.ShapeDtypeStruct((bands, 3 * bands), BF16),
            jax.ShapeDtypeStruct((8, bands), F32),
        ),
        in_specs=[far, far],
        out_specs=(vmem, vmem, vmem, vmem),
        scratch_shapes=[
            pltpu.VMEM((cx + 4, cy, cz, bands), BF16),
            pltpu.VMEM((cx, cy, cz), F32),
            pltpu.VMEM((cx, 2, cz, bands), BF16),
            pltpu.VMEM((cx, 2, cz, bands), BF16),
            pltpu.VMEM((cx, cy, 2, bands), BF16),
            pltpu.VMEM((cx, cy, 2, bands), BF16),
            pltpu.VMEM((2, cx, cy, 2, bands), BF16),
            dma((2,)), dma((6,)), dma((6,)),
            *reduce_scratch(sizes, bands, bands),
            *reduce_scratch(sizes, 2 * bands, bands),
        ],
        compiler_params=pltpu.CompilerParams(collective_id=0, has_side_effects=True, vmem_limit_bytes=48 * 1024 * 1024),
    )(wavefunctions, potential)
    steps = 8 if mine % 128 == 0 else 1
    tile = mine // steps
    block = pl.BlockSpec((tile, bands), lambda i: (i, 0))
    line = pl.BlockSpec((1, bands), lambda i: (0, 0))
    rotated, residual, quotients, norms = pl.pallas_call(
        finish_kernel,
        grid=(steps,),
        out_shape=(
            jax.ShapeDtypeStruct((mine, bands), F32),
            jax.ShapeDtypeStruct((mine, bands), BF16),
            jax.ShapeDtypeStruct((1, bands), F32),
            jax.ShapeDtypeStruct((1, bands), F32),
        ),
        in_specs=[pl.BlockSpec((bands, 3 * bands), lambda i: (0, 0)), pl.BlockSpec((8, bands), lambda i: (0, 0)),
                  block, block, block],
        out_specs=(block, block, line, line),
        compiler_params=pltpu.CompilerParams(vmem_limit_bytes=48 * 1024 * 1024),
    )(split, stats, wavefunctions.reshape(mine, bands), hi.reshape(mine, bands), lo.reshape(mine, bands))
    shape = wavefunctions.shape
    return rotated.reshape(shape), residual.reshape(shape), quotients.reshape(bands), norms.reshape(bands)


def solution(mesh):
    sizes = (mesh.shape["gx"], mesh.shape["gy"], mesh.shape["gz"])
    placed = (P("gx", "gy", "gz", None), P("gx", "gy", "gz"))
    return jax.shard_map(
        functools.partial(local, sizes),
        mesh=mesh,
        in_specs=placed,
        out_specs=(P("gx", "gy", "gz", None), P("gx", "gy", "gz", None), P(), P()),
        check_vma=False,
    )
```

time: 51.9 us -> 40.5 us (0.78)
  Pallas kernels: 48.9 us -> 37.6 us
    pallas_call x2, Pallas kernels: 48.9 us -> 37.6 us  [the longest x1 33.1 us: local(): pl.pallas_call(functools.partial(reduce_kernel, sizes, float(mine * nx *...]
where the time goes in v2:
time: 40.5 us; the launch traced here: 40.3 us
  Pallas kernels  37.6 us (93%)
  local copies, waits for them, and re-layouts  2.12 us (5%)
  between operations  0.65 us (2%)
    pallas_call x1, Pallas kernels, local(): pl.pallas_call(functools.partial(reduce_kernel, sizes, float(mine * nx *...  33.1 us
    pallas_call x1, Pallas kernels, local(): pl.pallas_call(finish_kernel, grid=(steps,), out_shape=(jax.ShapeDtypeStr...  4.52 us
    unnamed x4, local copies, waits for them, and re-layouts  2.12 us

profile of v2, /device:TPU:0, one launch (start us, length us, event | category | flops | bytes accessed | tf_op | source)
XLA Modules:
  0.0 40.3 jit_solution(8137413752190583342)
XLA Ops:
  0.6 0.0 copy-start
  0.6 1.2 %copy-done = bf16[16,16,16,128]{3,2,1,0:T(8,128)(2,1)S(1)} copy-done((bf16[16,16,16,128]{3,2,1,0:T(8,128)(2,1)S(1)}, bf16[16,16,16,128]{3,2,1,0:T(8,128)(2,1)}, u32[]{:S(2)}) %copy-start) | copy-done | bytes 1048600
  1.9 0.0 copy-start.1
  1.9 0.9 %copy-done.1 = f32[16,16,16]{2,1,0:T(8,128)S(1)} copy-done((f32[16,16,16]{2,1,0:T(8,128)S(1)}, f32[16,16,16]{2,1,0:T(8,128)}, u32[]{:S(2)}) %copy-start.1) | copy-done | bytes 16408
  2.8 33.1 %shard_map.57 = (bf16[16,16,16,128]{3,2,1,0:T(8,128)(2,1)S(1)}, bf16[16,16,16,128]{3,2,1,0:T(8,128)(2,1)S(1)}, bf16[128,384]{1,0:T(8,128)(2,1)S(1)}, f32[8,128]{1,0:T(8,128)S(1)}) custom-call(bf16[16,16,16,128]{3,2,1,0:T(8,128)(2,1)S(1)} %copy-done, f32[16,16,16]{2,1,0:T(8,128)S(1)} %copy-done.1), custom_call_target="tpu_custom_call" | custom-call | tf_op jit(solution)/shard_map/pallas_call | solution.py:276
  35.8 4.5 %shard_map.58 = (f32[4096,128]{1,0:T(8,128)}, bf16[4096,128]{1,0:T(8,128)(2,1)}, f32[1,128]{1,0:T(1,128)}, f32[1,128]{1,0:T(1,128)}) custom-call(bf16[128,384]{1,0:T(8,128)(2,1)S(1)} %get-tuple-element.12.split_ref, f32[8,128]{1,0:T(8,128)S(1)} %get-tuple-element.13.stats_ref, bf16[4096,128]{1,0:T(8,128)(2,1)S(1)} %bitcast.7, bf16[4096,128]{1,0:T(8,128)(2,1)S(1)} %bitcast.8, ...), custom_call_target="tpu_custom_call" | custom-call | tf_op jit(solution)/shard_map/pallas_call | solution.py:304
Async XLA Ops:
  0.6 1.2 %copy-start = (bf16[16,16,16,128]{3,2,1,0:T(8,128)(2,1)S(1)}, bf16[16,16,16,128]{3,2,1,0:T(8,128)(2,1)}, u32[]{:S(2)}) copy-start(bf16[16,16,16,128]{3,2,1,0:T(8,128)(2,1)} %p_any.1) | copy-start | bytes 3145732
  1.9 0.9 %copy-start.1 = (f32[16,16,16]{2,1,0:T(8,128)S(1)}, f32[16,16,16]{2,1,0:T(8,128)}, u32[]{:S(2)}) copy-start(f32[16,16,16]{2,1,0:T(8,128)} %v_any.1) | copy-start | bytes 49156

commit v3 on v2

--- a/solution.py
+++ b/solution.py
@@ -93,11 +93,10 @@
             self.gather_copy(o, lax.rem(self.my + self.ny - o, self.ny)).wait_recv()
 
 
-def reduce_scratch(sizes, rows, bands):
+def reduce_scratch(sizes, chunk, bands):
     nx, ny, nz = sizes
     ne = nx * nz
     dma = pltpu.SemaphoreType.DMA
-    chunk = rows // ny
     shapes = ((ny, chunk), (ny - 1, chunk), (chunk,), (ne, chunk), (chunk,), (ny, chunk))
     return [pltpu.VMEM(shape + (bands,), F32) for shape in shapes] + [dma((k - 1,)) for k in (ny, ny, ne, ne, ny, ny)]
 
@@ -133,8 +132,8 @@
     return out, rest
 
 
-def reduce_kernel(sizes, cells, p_any, v_any, hi_ref, lo_ref, split_ref, stats_ref,
-                  pext, vbuf, ylo, yhi, zlo, zhi, zsend, load_sem, hs, hr, *refs):
+def reduce_kernel(sizes, cells, p_any, v_any, rot_ref, app_ref, stats_ref,
+                  hi_ref, lo_ref, split_ref, pext, vbuf, ylo, yhi, zlo, zhi, zsend, load_sem, hs, hr, *refs):
     nx, ny, nz = sizes
     ne = nx * nz
     cx, cy, cz, bands = p_any.shape
@@ -151,17 +150,6 @@
     for o in range(1, ne):
         pl.semaphore_signal(barrier, inc=1, device_id=first.plane_peer(o), device_id_type=MESH)
     load.wait()
-    own = pext[2:2 + cx]
-    zsend[0] = own[:, :, cz - 2:, :]
-    zsend[1] = own[:, :, :2, :]
-    flat = own.reshape(cx * cy * cz, bands)
-    rows = bands // ny
-
-    def put(where, slot, matrix):
-        for k in range(ny):
-            where[k, slot * rows:(slot + 1) * rows] = matrix[k * rows:(k + 1) * rows]
-
-    put(first.part, 0, gram(flat, flat))
     pl.semaphore_wait(barrier, ny - 1 + ne - 1)
 
     def remote(src, dst, i, device):
@@ -174,20 +162,35 @@
     yb = (mx, lax.rem(my + ny - 1, ny), mz)
     zf = (mx, my, lax.rem(mz + 1, nz))
     zb = (mx, my, lax.rem(mz + nz - 1, nz))
-    halos = [
+    outer = [
+        remote(pext.at[pl.ds(cx, 2)], pext.at[pl.ds(0, 2)], 2, xf),
+        remote(pext.at[pl.ds(2, 2)], pext.at[pl.ds(cx + 2, 2)], 3, xb),
+    ]
+    inner = [
+        remote(pext.at[pl.ds(2, cx), pl.ds(cy - 2, 2)], ylo, 4, yf),
+        remote(pext.at[pl.ds(2, cx), pl.ds(0, 2)], yhi, 5, yb),
         remote(zsend.at[0], zlo, 0, zf),
         remote(zsend.at[1], zhi, 1, zb),
-        remote(pext.at[pl.ds(cx, 2)], pext.at[pl.ds(0, 2)], 2, xf),
-        remote(pext.at[pl.ds(2, 2)], pext.at[pl.ds(cx + 2, 2)], 3, xb),
-        remote(pext.at[pl.ds(2, cx), pl.ds(cy - 2, 2)], ylo, 4, yf),
-        remote(pext.at[pl.ds(2, cx), pl.ds(0, 2)], yhi, 5, yb),
     ]
+    for copy in inner[:2] + outer:
+        copy.start()
+    own = pext[2:2 + cx]
+    zsend[0] = own[:, :, cz - 2:, :]
+    zsend[1] = own[:, :, :2, :]
+    for copy in inner[2:]:
+        copy.start()
+    rows = bands // ny
+
+    def cells_of(ref, start, stop):
+        return ref[start:stop].reshape((stop - start) * cy * cz, bands)
+
+    flat = cells_of(pext, 2, 2 + cx)
+    matrix = gram(flat, flat)
+    for k in range(ny):
+        first.part[k] = matrix[k * rows:(k + 1) * rows]
     first.scatter()
-    for copy in halos:
-        copy.start()
     load_v.wait()
-    first.exchange()
-    for copy in halos:
+    for copy in inner:
         copy.wait()
 
     def plane(i, carry):
@@ -208,13 +211,28 @@
         lo_ref[i] = lo
         return carry
 
-    lax.fori_loop(0, cx, plane, 0)
-    flat = pext[2:2 + cx].reshape(cx * cy * cz, bands)
-    hi = hi_ref[...].reshape(cx * cy * cz, bands)
-    lo = lo_ref[...].reshape(cx * cy * cz, bands)
-    put(second.part, 0, gram(flat, hi) + gram(flat, lo))
-    cross = gram(hi, lo)
-    put(second.part, 1, gram(hi, hi) + cross + cross.T)
+    lax.fori_loop(2, cx - 2, plane, 0)
+    first.exchange()
+
+    def grams(start, stop):
+        p = cells_of(pext, 2 + start, 2 + stop)
+        hi, lo = cells_of(hi_ref, start, stop), cells_of(lo_ref, start, stop)
+        return gram(p, hi) + gram(p, lo), gram(hi, hi), gram(hi, lo)
+
+    most = grams(2, cx - 2)
+    for copy in outer:
+        copy.wait()
+    for i in (0, 1, cx - 2, cx - 1):
+        plane(i, 0)
+    cross, square, mixed = [a + b + c for a, b, c in zip(most, grams(0, 2), grams(cx - 2, cx))]
+    square = square + mixed + mixed.T
+    row = lax.broadcasted_iota(jnp.int32, (bands, bands), 0)
+    col = lax.broadcasted_iota(jnp.int32, (bands, bands), 1)
+    diagonal = jnp.sum(jnp.where(row == col, cross, 0.0), axis=0, keepdims=True)
+    packed = jnp.where(row < col, cross + cross.T, jnp.where(row > col, 2.0 * square, square))
+    for k in range(ny):
+        second.part[k, :rows] = packed[k * rows:(k + 1) * rows]
+        second.part[k, rows:] = jnp.broadcast_to(diagonal, (8, bands))
     second.scatter()
     first.gather()
     second.exchange()
@@ -226,13 +244,27 @@
     tiles = [matrix[8 * t:8 * t + 8] for t in range(count)]
     inverse = []
     for t in range(count):
-        if t == count * 3 // 4:
-            second.gather()
         out, tiles = eliminate(tiles, t)
         inverse.append(out)
     inverse_t = jnp.concatenate(inverse, axis=0).T
     for i, piece in enumerate(split3(inverse_t)):
         split_ref[:, i * bands:(i + 1) * bands] = piece
+    second.gather()
+    planes = 4 if cx % 4 == 0 else 1
+
+    def rotate(i, carry):
+        at = pl.ds(i * planes, planes)
+        shape = (planes * cy * cz, bands)
+        split = split_ref[...]
+        p = pext[pl.ds(i * planes + 2, planes)].reshape(shape)
+        wide = dot(p, split[:, :2 * bands])
+        rot_ref[at] = (wide[:, :bands] + (wide[:, bands:] + dot(p, split[:, 2 * bands:]))).reshape(planes, cy, cz, bands)
+        wide = dot(hi_ref[at].reshape(shape), split[:, :2 * bands])
+        applied = wide[:, :bands] + (wide[:, bands:] + dot(lo_ref[at].reshape(shape), split[:, :bands]))
+        app_ref[at] = applied.reshape(planes, cy, cz, bands)
+        return carry
+
+    lax.fori_loop(0, cx // planes, rotate, 0)
     second.finish()
 
     def quadratic(m):
@@ -240,8 +272,10 @@
         return jnp.sum(inverse_t * prod, axis=0, keepdims=True)
 
     rotated_all = quadratic(correlation)
-    cross_all = quadratic(second.gathered[:, :rows].reshape(bands, bands))
-    applied_all = quadratic(second.gathered[:, rows:].reshape(bands, bands))
+    sums = second.gathered[:, :rows].reshape(bands, bands)
+    diagonal = second.gathered[0, rows:rows + 1]
+    cross_all = quadratic(jnp.where(row < col, sums, jnp.where(row == col, diagonal, 0.0)))
+    applied_all = quadratic(jnp.where(row < col, 0.0, sums))
     quotients = cross_all / cells
     squares = applied_all - 2.0 * quotients * cross_all + quotients * quotients * rotated_all
     stats_ref[0:1] = quotients
@@ -252,16 +286,10 @@
     return jnp.dot(a, b, preferred_element_type=F32)
 
 
-def finish_kernel(split_ref, stats_ref, p_ref, hi_ref, lo_ref, rot_ref, res_ref, quo_ref, norm_ref):
-    bands = p_ref.shape[1]
-    split = split_ref[...]
-    p = p_ref[...]
-    wide = dot(p, split[:, :2 * bands])
-    rotated = wide[:, :bands] + (wide[:, bands:] + dot(p, split[:, 2 * bands:]))
+def finish_kernel(stats_ref, given_ref, app_ref, rot_ref, res_ref, quo_ref, norm_ref):
+    rotated = given_ref[...]
     rot_ref[...] = rotated
-    wide = dot(hi_ref[...], split[:, :2 * bands])
-    applied = wide[:, :bands] + (wide[:, bands:] + dot(lo_ref[...], split[:, :bands]))
-    res_ref[...] = (applied - stats_ref[0:1] * rotated).astype(BF16)
+    res_ref[...] = (app_ref[...] - stats_ref[0:1] * rotated).astype(BF16)
     quo_ref[...] = stats_ref[0:1]
     norm_ref[...] = stats_ref[1:2]
 
@@ -273,17 +301,19 @@
     vmem = pl.BlockSpec(memory_space=pltpu.VMEM)
     far = pl.BlockSpec(memory_space=pltpu.HBM)
     dma = pltpu.SemaphoreType.DMA
-    hi, lo, split, stats = pl.pallas_call(
+    rotated, applied, stats = pl.pallas_call(
         functools.partial(reduce_kernel, sizes, float(mine * nx * ny * nz)),
         out_shape=(
-            jax.ShapeDtypeStruct(wavefunctions.shape, BF16),
-            jax.ShapeDtypeStruct(wavefunctions.shape, BF16),
-            jax.ShapeDtypeStruct((bands, 3 * bands), BF16),
+            jax.ShapeDtypeStruct(wavefunctions.shape, F32),
+            jax.ShapeDtypeStruct(wavefunctions.shape, F32),
             jax.ShapeDtypeStruct((8, bands), F32),
         ),
         in_specs=[far, far],
-        out_specs=(vmem, vmem, vmem, vmem),
+        out_specs=(vmem, vmem, vmem),
         scratch_shapes=[
+            pltpu.VMEM(wavefunctions.shape, BF16),
+            pltpu.VMEM(wavefunctions.shape, BF16),
+            pltpu.VMEM((bands, 3 * bands), BF16),
             pltpu.VMEM((cx + 4, cy, cz, bands), BF16),
             pltpu.VMEM((cx, cy, cz), F32),
             pltpu.VMEM((cx, 2, cz, bands), BF16),
@@ -292,8 +322,8 @@
             pltpu.VMEM((cx, cy, 2, bands), BF16),
             pltpu.VMEM((2, cx, cy, 2, bands), BF16),
             dma((2,)), dma((6,)), dma((6,)),
-            *reduce_scratch(sizes, bands, bands),
-            *reduce_scratch(sizes, 2 * bands, bands),
+            *reduce_scratch(sizes, bands // ny, bands),
+            *reduce_scratch(sizes, bands // ny + 8, bands),
         ],
         compiler_params=pltpu.CompilerParams(collective_id=0, has_side_effects=True, vmem_limit_bytes=48 * 1024 * 1024),
     )(wavefunctions, potential)
@@ -310,11 +340,10 @@
             jax.ShapeDtypeStruct((1, bands), F32),
             jax.ShapeDtypeStruct((1, bands), F32),
         ),
-        in_specs=[pl.BlockSpec((bands, 3 * bands), lambda i: (0, 0)), pl.BlockSpec((8, bands), lambda i: (0, 0)),
-                  block, block, block],
+        in_specs=[pl.BlockSpec((8, bands), lambda i: (0, 0)), block, block],
         out_specs=(block, block, line, line),
         compiler_params=pltpu.CompilerParams(vmem_limit_bytes=48 * 1024 * 1024),
-    )(split, stats, wavefunctions.reshape(mine, bands), hi.reshape(mine, bands), lo.reshape(mine, bands))
+    )(stats, rotated.reshape(mine, bands), applied.reshape(mine, bands))
     shape = wavefunctions.shape
     return rotated.reshape(shape), residual.reshape(shape), quotients.reshape(bands), norms.reshape(bands)
 

time: 40.5 us -> 37.3 us (0.921)
  Pallas kernels: 37.6 us -> 34.4 us
    pallas_call x1, Pallas kernels: 33.1 us -> 31.1 us  [local(): pl.pallas_call(functools.partial(reduce_kernel, sizes, float(mine * nx *...]
    pallas_call x1, Pallas kernels: 4.52 us -> 3.27 us  [local(): pl.pallas_call(finish_kernel, grid=(steps,), out_shape=(jax.ShapeDtypeStr...]
where the time goes in v3:
time: 37.3 us; the launch traced here: 37.2 us
  Pallas kernels  34.4 us (92%)
  local copies, waits for them, and re-layouts  2.12 us (6%)
  between operations  0.65 us (2%)
    pallas_call x1, Pallas kernels, local(): pl.pallas_call(functools.partial(reduce_kernel, sizes, float(mine * nx *...  31.1 us
    pallas_call x1, Pallas kernels, local(): pl.pallas_call(finish_kernel, grid=(steps,), out_shape=(jax.ShapeDtypeStr...  3.27 us
    unnamed x4, local copies, waits for them, and re-layouts  2.12 us

profile of v3, /device:TPU:0, one launch (start us, length us, event | category | flops | bytes accessed | tf_op | source)
XLA Modules:
  0.0 37.2 jit_solution(11992424141313547724)
XLA Ops:
  0.6 0.0 copy-start
  0.6 1.2 %copy-done = bf16[16,16,16,128]{3,2,1,0:T(8,128)(2,1)S(1)} copy-done((bf16[16,16,16,128]{3,2,1,0:T(8,128)(2,1)S(1)}, bf16[16,16,16,128]{3,2,1,0:T(8,128)(2,1)}, u32[]{:S(2)}) %copy-start) | copy-done | bytes 1048600
  1.9 0.0 copy-start.1
  1.9 0.9 %copy-done.1 = f32[16,16,16]{2,1,0:T(8,128)S(1)} copy-done((f32[16,16,16]{2,1,0:T(8,128)S(1)}, f32[16,16,16]{2,1,0:T(8,128)}, u32[]{:S(2)}) %copy-start.1) | copy-done | bytes 16408
  2.8 31.1 %shard_map.57 = (f32[16,16,16,128]{3,2,1,0:T(8,128)S(1)}, f32[16,16,16,128]{3,2,1,0:T(8,128)S(1)}, f32[8,128]{1,0:T(8,128)S(1)}) custom-call(bf16[16,16,16,128]{3,2,1,0:T(8,128)(2,1)S(1)} %copy-done, f32[16,16,16]{2,1,0:T(8,128)S(1)} %copy-done.1), custom_call_target="tpu_custom_call" | custom-call | tf_op jit(solution)/shard_map/pallas_call | solution.py:304
  33.9 3.3 %shard_map.58 = (f32[4096,128]{1,0:T(8,128)}, bf16[4096,128]{1,0:T(8,128)(2,1)}, f32[1,128]{1,0:T(1,128)}, f32[1,128]{1,0:T(1,128)}) custom-call(f32[8,128]{1,0:T(8,128)S(1)} %get-tuple-element.11.stats_ref, f32[4096,128]{1,0:T(8,128)S(1)} %bitcast.6, f32[4096,128]{1,0:T(8,128)S(1)} %bitcast.7), custom_call_target="tpu_custom_call" | custom-call | tf_op jit(solution)/shard_map/pallas_call | solution.py:334
Async XLA Ops:
  0.6 1.2 %copy-start = (bf16[16,16,16,128]{3,2,1,0:T(8,128)(2,1)S(1)}, bf16[16,16,16,128]{3,2,1,0:T(8,128)(2,1)}, u32[]{:S(2)}) copy-start(bf16[16,16,16,128]{3,2,1,0:T(8,128)(2,1)} %p_any.1) | copy-start | bytes 3145732
  1.9 0.9 %copy-start.1 = (f32[16,16,16]{2,1,0:T(8,128)S(1)}, f32[16,16,16]{2,1,0:T(8,128)}, u32[]{:S(2)}) copy-start(f32[16,16,16]{2,1,0:T(8,128)} %v_any.1) | copy-start | bytes 49156

commit v4 on v3

--- a/solution.py
+++ b/solution.py
@@ -327,7 +327,7 @@
         ],
         compiler_params=pltpu.CompilerParams(collective_id=0, has_side_effects=True, vmem_limit_bytes=48 * 1024 * 1024),
     )(wavefunctions, potential)
-    steps = 8 if mine % 128 == 0 else 1
+    steps = 2 if mine % 128 == 0 else 1
     tile = mine // steps
     block = pl.BlockSpec((tile, bands), lambda i: (i, 0))
     line = pl.BlockSpec((1, bands), lambda i: (0, 0))

time: 37.3 us -> 35.9 us (0.962)
  Pallas kernels: 34.4 us -> 33 us
    pallas_call x1, Pallas kernels: 3.27 us -> 1.87 us  [local(): pl.pallas_call(finish_kernel, grid=(steps,), out_shape=(jax.ShapeDtypeStr...]
where the time goes in v4:
time: 35.9 us; the launch traced here: 35.8 us
  Pallas kernels  33 us (92%)
  local copies, waits for them, and re-layouts  2.12 us (6%)
  between operations  0.65 us (2%)
    pallas_call x1, Pallas kernels, local(): pl.pallas_call(functools.partial(reduce_kernel, sizes, float(mine * nx *...  31.1 us
    unnamed x4, local copies, waits for them, and re-layouts  2.12 us
    pallas_call x1, Pallas kernels, local(): pl.pallas_call(finish_kernel, grid=(steps,), out_shape=(jax.ShapeDtypeStr...  1.87 us

profile of v4, /device:TPU:0, one launch (start us, length us, event | category | flops | bytes accessed | tf_op | source)
XLA Modules:
  0.0 35.8 jit_solution(3592457514019054344)
XLA Ops:
  0.6 0.0 copy-start
  0.6 1.2 %copy-done = bf16[16,16,16,128]{3,2,1,0:T(8,128)(2,1)S(1)} copy-done((bf16[16,16,16,128]{3,2,1,0:T(8,128)(2,1)S(1)}, bf16[16,16,16,128]{3,2,1,0:T(8,128)(2,1)}, u32[]{:S(2)}) %copy-start) | copy-done | bytes 1048600
  1.9 0.0 copy-start.1
  1.9 0.9 %copy-done.1 = f32[16,16,16]{2,1,0:T(8,128)S(1)} copy-done((f32[16,16,16]{2,1,0:T(8,128)S(1)}, f32[16,16,16]{2,1,0:T(8,128)}, u32[]{:S(2)}) %copy-start.1) | copy-done | bytes 16408
  2.8 31.1 %shard_map.57 = (f32[16,16,16,128]{3,2,1,0:T(8,128)S(1)}, f32[16,16,16,128]{3,2,1,0:T(8,128)S(1)}, f32[8,128]{1,0:T(8,128)S(1)}) custom-call(bf16[16,16,16,128]{3,2,1,0:T(8,128)(2,1)S(1)} %copy-done, f32[16,16,16]{2,1,0:T(8,128)S(1)} %copy-done.1), custom_call_target="tpu_custom_call" | custom-call | tf_op jit(solution)/shard_map/pallas_call | solution.py:304
  33.9 1.9 %shard_map.58 = (f32[4096,128]{1,0:T(8,128)}, bf16[4096,128]{1,0:T(8,128)(2,1)}, f32[1,128]{1,0:T(1,128)}, f32[1,128]{1,0:T(1,128)}) custom-call(f32[8,128]{1,0:T(8,128)S(1)} %get-tuple-element.11.stats_ref, f32[4096,128]{1,0:T(8,128)S(1)} %bitcast.6, f32[4096,128]{1,0:T(8,128)S(1)} %bitcast.7), custom_call_target="tpu_custom_call" | custom-call | tf_op jit(solution)/shard_map/pallas_call | solution.py:334
Async XLA Ops:
  0.6 1.2 %copy-start = (bf16[16,16,16,128]{3,2,1,0:T(8,128)(2,1)S(1)}, bf16[16,16,16,128]{3,2,1,0:T(8,128)(2,1)}, u32[]{:S(2)}) copy-start(bf16[16,16,16,128]{3,2,1,0:T(8,128)(2,1)} %p_any.1) | copy-start | bytes 3145732
  1.9 0.9 %copy-start.1 = (f32[16,16,16]{2,1,0:T(8,128)S(1)}, f32[16,16,16]{2,1,0:T(8,128)}, u32[]{:S(2)}) copy-start(f32[16,16,16]{2,1,0:T(8,128)} %v_any.1) | copy-start | bytes 49156
